TPU v7x, 32 devices: a whole 2x2x4 slice. The times are simulated.
32 devices in a mesh: ao: 4 (over z), gen: 4 (over y, core), act: 2 (over x).
Axes of the slice: x: 2, y: 2, z: 4, core: 2. Of those that a mesh axis runs over, the one named last changes fastest.
Arguments:
- integrals: bfloat16 [384, 2, 128, 1152], P(('ao', 'gen', 'act')), may hold values from -6 to 6
- bra_rows: bfloat16 [384, 2, 128, 16], P(('ao', 'gen', 'act')), may hold values from -0.02734375 to 0.02734375
- ket_rows: bfloat16 [384, 2, 128, 48], P(('ao', 'gen', 'act')), may hold values from -6 to 6
- block_count: int32 [32], P(('ao', 'gen', 'act')), may hold values from 1 to 12, as said below
- pair_count: int32 [384], P(('ao', 'gen', 'act')), may hold values from 32 to 128
Outputs:
- transformed: float32 [2, 16, 48, 1152], P(None, 'gen', 'act', 'ao')
Inputs may be any that keep to these rules, and one draw needn't show every extreme that they name: `block_count`: one device holds exactly 12 live blocks. Rows from pair_count on are padding.
All inputs are finite; a program needn't handle non-finite values.
Results may differ from a plain program's by a relative error of at most 0.0042.
Values may be sent and summed in bfloat16 or wider, within the bound.
No kernel may reach another device: no remote copies, remote signals or barrier semaphores. Data moves between devices by JAX's collectives and lax.ppermute only.
A program may use at most 128 MiB of HBM per device.

v0:
```python
import functools

import jax
import jax.numpy as jnp
from jax import lax
from jax.experimental import pallas as pl
from jax.experimental.pallas import tpu as pltpu
from jax.sharding import PartitionSpec as P


LANES = 128
GRAIN = 8
STEP = 2
VMEM_BYTES = 67043328
SLACK = 12*2**20
SMALL = 4 * 2**20
STAGES = ((("far", 1, 1), ("near", 1, 0)), (("two", 0, 1), ("own", 0, 0)))


def parts_of(p_own):
    return (p_own // 2, p_own // 2) if p_own % 2 == 0 else (p_own,)


def make_weights(dims, wave, t, left, bra_pack, ket_pack, weights):
    general, active, gen_size, act_size = dims
    p_own, u_own = general // gen_size, active // act_size
    me_gen, me_act = lax.axis_index("gen"), lax.axis_index("act")
    right = left + 1
    row = 0
    for core in (1, 0):
        odd = (me_gen & 1) ^ core
        for _, first, second in STAGES[wave]:
            q = jnp.where(odd == 1, first, second)
            a = jnp.where(odd == 1, second, first)
            p_first = (me_gen ^ (2 * q + core)) * p_own
            u_first = pl.multiple_of((me_act ^ a) * u_own, 8)
            ket_re = ket_pack[t, pl.ds(u_first, u_own), :]
            ket_im = ket_pack[t, pl.ds(active + u_first, u_own), :]
            p_from = 0
            for part in parts_of(p_own):
                real, imag = [], []
                for p in range(p_from, p_from + part):
                    bra_re = bra_pack[t, pl.ds(p_first + p, 1), :]
                    bra_im = bra_pack[t, pl.ds(general + p_first + p, 1), :]
                    real.append(bra_re * ket_re + bra_im * ket_im)
                    imag.append(bra_re * ket_im - bra_im * ket_re)
                p_from += part
                size = part * u_own
                real = jnp.concatenate(real, axis=0)
                imag = jnp.concatenate(imag, axis=0)
                real_low = real.astype(jnp.bfloat16)
                weights[left, row : row + size] = real_low
                weights[right, row : row + size] = (-imag).astype(jnp.bfloat16)
                row += size
                weights[left, row : row + size] = imag.astype(jnp.bfloat16)
                weights[right, row : row + size] = real_low
                row += size


def accumulate(dims, chunk, tiles, packed, bra_pack, ket_pack, weights, acc, results, arrive):
    def product(first, count, state):
        for k in range(count):
            make_weights(dims, chunk, first + k, 2 * k, bra_pack, ket_pack, weights)
        state = arrive(first + count, state)
        values = []
        for k in range(count):
            row = pl.multiple_of((first + k) * LANES, LANES)
            values.append(packed[0, pl.ds(row, LANES), :])
            values.append(packed[1, pl.ds(row, LANES), :])
        values = jnp.concatenate(values, axis=0)
        left = jnp.concatenate([weights[k] for k in range(2 * count)], axis=1)
        return jnp.dot(left, values, preferred_element_type=jnp.float32), state

    def step(i, state):
        value, state = product(i * STEP, STEP, state)
        acc[...] += value
        return state

    steps = (tiles - 1) // STEP

    def opening(state):
        value, state = product(0, STEP, state)
        acc[...] = value
        return state

    def empty(state):
        acc[...] = jnp.zeros_like(acc)
        return state

    state = lax.cond(steps > 0, opening, empty, 0)
    state = lax.fori_loop(1, steps, step, state)
    for count in range(1, STEP + 1):
        @pl.when(tiles - steps * STEP == count)
        def _():
            value, _ = product(steps * STEP, count, state)
            value = acc[...] + value
            row = 0
            for result in results:
                result[...] = value[row : row + result.shape[0]].astype(result.dtype)
                row += result.shape[0]


def head_kernel(dims, blocks, width, rows_ref, ints_ref, *refs):
    *results, packed, bra_pack, ket_pack = refs[:-5]
    weights, acc, counts, offsets, sems = refs[-5:]
    general = dims[0]

    def rows_of(b):
        return (counts[b] + GRAIN - 1) // GRAIN * GRAIN

    pieces = []
    size = width
    while size >= GRAIN:
        pieces.append(size)
        size //= 2

    def pieced(b, rows, start, piece):
        first = pl.multiple_of(rows & ~(2 * piece - 1), GRAIN)
        return pltpu.make_async_copy(
            ints_ref.at[b, :, pl.ds(first, piece), :],
            packed.at[:, pl.ds(start + first, piece), :],
            sems.at[b],
        )

    total = 0
    for b in range(blocks):
        marks = rows_ref[b, 0, rows_ref.shape[2] - 8 :].astype(jnp.float32)
        counts[b] = jnp.max(marks).astype(jnp.int32)
        rows = rows_of(b)
        offsets[b] = total
        start = pl.multiple_of(total, GRAIN)
        for piece in pieces:
            @pl.when((rows & piece) != 0)
            def _():
                pieced(b, rows, start, piece).start()

        total = total + rows
    tiles = (total + LANES - 1) // LANES

    def clear(i, _):
        row = pl.multiple_of(total + i * GRAIN, GRAIN)
        packed[:, pl.ds(row, GRAIN), :] = jnp.zeros((2, GRAIN, packed.shape[2]), packed.dtype)
        return 0

    lax.fori_loop(0, (tiles * LANES - total) // GRAIN, clear, 0)

    @pl.loop(0, tiles + 1)
    def _(t):
        bra_pack[t] = jnp.zeros(bra_pack.shape[1:], jnp.float32)
        ket_pack[t] = jnp.zeros(ket_pack.shape[1:], jnp.float32)

    bra_pack[bra_pack.shape[0] - 1] = jnp.full(
        bra_pack.shape[1:], tiles.astype(jnp.float32), jnp.float32
    )
    lane = lax.broadcasted_iota(jnp.int32, (1, LANES), 1)
    for b in range(blocks):
        start = offsets[b]
        rows = counts[b]
        tile = start // LANES
        turn = start % LANES
        both = rows_ref[b].astype(jnp.float32)
        for first, last, target in ((0, general, bra_pack), (general, both.shape[1] - 8, ket_pack)):
            value = both[:, first:last].reshape(target.shape[1:])
            value = pltpu.roll(jnp.where(lane < rows, value, 0.0), turn, 1)
            target[tile] += jnp.where(lane >= turn, value, 0.0)
            target[tile + 1] += jnp.where(lane < turn, value, 0.0)

    def arrive(until, ready):
        def pending(b):
            start = offsets[jnp.minimum(b, blocks - 1)]
            return jnp.logical_and(b < blocks, start < jnp.minimum(until * LANES, total))

        def wait(b):
            rows = rows_of(b)
            start = pl.multiple_of(offsets[b], GRAIN)
            for piece in pieces:
                @pl.when((rows & piece) != 0)
                def _():
                    pieced(b, rows, start, piece).wait()

            return b + 1

        return lax.while_loop(pending, wait, ready)

    accumulate(dims, 0, tiles, packed, bra_pack, ket_pack, weights, acc, results, arrive)


def tail_kernel(dims, chunk, packed, bra_pack, ket_pack, *refs):
    *results, weights, acc = refs
    tiles = jnp.max(bra_pack[bra_pack.shape[0] - 1, :8]).astype(jnp.int32)
    accumulate(
        dims, chunk, tiles, packed, bra_pack, ket_pack, weights, acc, results,
        lambda until, state: state,
    )


SMEM = pl.BlockSpec(memory_space=pltpu.SMEM)
VMEM = pl.BlockSpec(memory_space=pltpu.VMEM)
HBM = pl.BlockSpec(memory_space=pltpu.HBM)


def products(dims, chunk, operands):
    general, active, gen_size, act_size = dims
    columns = operands[-1].shape[3] if chunk == 0 else operands[0].shape[2]
    blocks = operands[0].shape[0]
    blocks_rows = [2 * part * (active // act_size) for part in parts_of(general // gen_size)]
    half = sum(blocks_rows)
    rows = 2 * half * len(STAGES[chunk])
    outs = [jax.ShapeDtypeStruct((half, columns), jnp.bfloat16) for _ in STAGES[chunk]]
    outs += [
        jax.ShapeDtypeStruct((size, columns), jnp.float32)
        for _ in STAGES[chunk]
        for size in blocks_rows
    ]
    out_specs = [VMEM] * len(outs)
    work = [
        pltpu.VMEM((2 * STEP, rows, LANES), jnp.bfloat16),
        pltpu.VMEM((rows, columns), jnp.float32),
    ]
    cost = pl.CostEstimate(
        flops=rows * columns * 2 * blocks * LANES, bytes_accessed=rows * columns * 3, transcendentals=0
    )
    if chunk:
        return pl.pallas_call(
            functools.partial(tail_kernel, dims, chunk),
            out_shape=outs,
            in_specs=[VMEM, VMEM, VMEM],
            out_specs=out_specs,
            scratch_shapes=work,
            compiler_params=pltpu.CompilerParams(vmem_limit_bytes=16 * 2**20),
            cost_estimate=cost,
        )(*operands)
    _, integrals = operands
    width = integrals.shape[2]
    tiles = -(-blocks * width // LANES)
    outs += [
        jax.ShapeDtypeStruct((2, tiles * LANES, columns), jnp.bfloat16),
        jax.ShapeDtypeStruct((tiles + 2, 2 * general, LANES), jnp.float32),
        jax.ShapeDtypeStruct((tiles + 1, 2 * active, LANES), jnp.float32),
    ]
    grant = VMEM_BYTES - sum(x.size * x.dtype.itemsize for x in outs) - SLACK
    return pl.pallas_call(
        functools.partial(head_kernel, dims, blocks, width),
        out_shape=outs,
        in_specs=[VMEM, HBM],
        out_specs=[VMEM] * len(outs),
        scratch_shapes=[
            *work,
            pltpu.SMEM((blocks,), jnp.int32),
            pltpu.SMEM((blocks,), jnp.int32),
            pltpu.SemaphoreType.DMA((blocks,)),
        ],
        compiler_params=pltpu.CompilerParams(vmem_limit_bytes=grant),
        cost_estimate=cost,
        name="products_0",
    )(*operands)


def window_of(columns, parts):
    own = columns // parts
    starts = [own * a // LANES * LANES for a in range(parts)]
    ends = [-(-own * (a + 1) // LANES) * LANES for a in range(parts)]
    return own, max(e - s for s, e in zip(starts, ends))


def dense_rows(own, rows):
    full, rest = divmod(own, LANES)
    return full * rows + rows * rest // LANES


def small(kernel, outs, *operands):
    return pl.pallas_call(
        kernel,
        out_shape=outs,
        in_specs=[VMEM] * len(operands),
        out_specs=jax.tree.map(lambda _: VMEM, outs),
        compiler_params=pltpu.CompilerParams(vmem_limit_bytes=SMALL),
        cost_estimate=pl.CostEstimate(
            flops=sum(x.size for x in operands),
            bytes_accessed=4 * sum(x.size for x in operands),
            transcendentals=0,
        ),
    )(*operands)


def total_call(kernel, outs, shape, *operands):
    scratch = [pltpu.VMEM(shape, jnp.float32)] if outs else []
    outs = outs or [jax.ShapeDtypeStruct(shape, jnp.float32)]
    return pl.pallas_call(
        kernel,
        out_shape=outs,
        in_specs=[VMEM] * len(operands),
        out_specs=[VMEM] * len(outs),
        scratch_shapes=scratch,
        compiler_params=pltpu.CompilerParams(vmem_limit_bytes=SMALL),
        cost_estimate=pl.CostEstimate(
            flops=sum(x.size for x in operands),
            bytes_accessed=4 * sum(x.size for x in operands),
            transcendentals=0,
        ),
    )(*operands)


def far_kernel(*refs):
    *kept, got_ref, out = refs
    row = 0
    for ref in kept:
        last = row + ref.shape[0]
        value = ref[...] + got_ref[row:last].astype(jnp.float32)
        out[row:last] = value.astype(out.dtype)
        row = last


def near_kernel(row, kept_ref, got_ref, out):
    last = row + kept_ref.shape[0]
    out[...] = (kept_ref[...] + got_ref[row:last].astype(jnp.float32)).astype(out.dtype)


def two_kernel(row, kept_ref, got_ref, from_far, out):
    last = row + kept_ref.shape[0]
    value = kept_ref[...] + got_ref[row:last].astype(jnp.float32)
    out[...] = (value + from_far[row:last].astype(jnp.float32)).astype(out.dtype)


def total_kernel(row, parts, own_ref, got_ref, from_near, from_two, *outs):
    total = outs[-1]
    last = row + own_ref.shape[0]
    value = own_ref[...] + got_ref[row:last].astype(jnp.float32)
    total[...] = value + from_near[...].astype(jnp.float32) + from_two[...].astype(jnp.float32)
    if parts:
        rows, columns = total.shape
        own, width = window_of(columns, parts)
        full, rest = divmod(own, LANES)
        lane = lax.broadcasted_iota(jnp.int32, (1, LANES), 1)
        me = lax.axis_index("ao")
        for k, out in enumerate(outs[:-1]):
            first = jnp.minimum((me ^ k) * own // LANES * LANES, columns - width)
            shift = (me ^ k) * own - first
            cut = total[:, pl.ds(pl.multiple_of(first, LANES), width)]
            cut = pltpu.roll(cut, jnp.where(shift == 0, 0, width - shift), 1)
            parcels = [cut[:, j * LANES : (j + 1) * LANES] for j in range(full)]
            if rest:
                groups = LANES // rest
                size = rows // groups
                left = cut[:, full * LANES : (full + 1) * LANES]
                parcel = left[:size]
                for g in range(1, groups):
                    moved = pltpu.roll(left[g * size : (g + 1) * size], g * rest, 1)
                    parcel = jnp.where(lane >= g * rest, moved, parcel)
                parcels.append(parcel)
            out[...] = jnp.concatenate(parcels, axis=0).astype(out.dtype)


def final_kernel(parts, own, *refs):
    out_ref = refs[-1]
    u_own = out_ref.shape[2]
    full, rest = divmod(own, LANES)
    p_from = 0
    for j in range(len(refs) // parts):
        group = refs[j * parts : (j + 1) * parts]
        value = group[0][...]
        for ref in group[1:]:
            value = value + ref[...].astype(jnp.float32)
        rows = value.shape[0] * LANES // own
        pieces = [value[i * rows : (i + 1) * rows] for i in range(full)]
        if rest:
            left = value[full * rows :]
            turns = [left] + [
                pltpu.roll(left, LANES - g * rest, 1) for g in range(1, LANES // rest)
            ]
            pieces.append(jnp.concatenate(turns, axis=0))
        value = jnp.concatenate(pieces, axis=1)[:, :own]
        part = rows // (2 * u_own)
        out_ref[:, p_from : p_from + part] = value.reshape(2, part, u_own, own)
        p_from += part


def swap(size, bit):
    return [(i, i ^ bit) for i in range(size)]


def local(integrals, bra_rows, ket_rows, block_count, pair_count):
    columns = integrals.shape[3]
    general, active = bra_rows.shape[3], ket_rows.shape[3]
    ao_size = lax.axis_size("ao")
    gen_size = lax.axis_size("gen")
    act_size = lax.axis_size("act")
    bra = jnp.swapaxes(bra_rows, 2, 3)
    ket = jnp.swapaxes(ket_rows, 2, 3)
    p_own, u_own = general // gen_size, active // act_size
    dims = (general, active, gen_size, act_size)
    blocks, _, width, _ = integrals.shape
    assert width <= 256
    live = jnp.where(jnp.arange(blocks, dtype=jnp.int32) < block_count, pair_count, 0)
    tail = jnp.broadcast_to(live.astype(bra.dtype)[:, None, None, None], (blocks, 2, 8, width))
    operands = (jnp.concatenate([bra, ket, tail], axis=2), integrals)
    own, width = window_of(columns, ao_size)
    outs = []
    assert (gen_size, act_size) == (4, 2)
    sizes = [2 * part * u_own for part in parts_of(p_own)]
    low = [jax.ShapeDtypeStruct((size, columns), jnp.bfloat16) for size in sizes]

    def move(value, axis, bit):
        return lax.ppermute(value, axis, swap(lax.axis_size(axis), bit))

    def cross(value, odd_first):
        def partner(g, k):
            return (g ^ 2, k) if g % 2 == odd_first else (g, k ^ 1)

        pairs = []
        for g in range(gen_size):
            for k in range(act_size):
                to_g, to_k = partner(g, k)
                pairs.append((g * act_size + k, to_g * act_size + to_k))
        return lax.ppermute(value, ("gen", "act"), pairs)

    kept, got = {}, {}
    for wave, stages in enumerate(STAGES):
        made = list(products(dims, wave, operands))
        for name, _, _ in stages:
            got[name] = move(made.pop(0), "gen", 1)
        for name, _, _ in stages:
            kept[name] = [made.pop(0) for _ in sizes]
        if wave == 0:
            operands = tuple(made)
            whole = jax.ShapeDtypeStruct((sum(sizes), columns), jnp.bfloat16)
            value = small(far_kernel, whole, *kept["far"], got["far"])
            from_far = cross(value, 1)
    parts = ao_size if ao_size <= 4 else 0
    outs = []
    row = 0
    for j, size in enumerate(sizes):
        value = small(
            functools.partial(near_kernel, row), low[j],
            kept["near"][j], got["near"],
        )
        from_near = cross(value, 1)
        value = small(
            functools.partial(two_kernel, row), low[j],
            kept["two"][j], got["two"], from_far,
        )
        from_two = cross(value, 0)
        totals = [
            jax.ShapeDtypeStruct((dense_rows(own, size), LANES), jnp.bfloat16 if k else jnp.float32)
            for k in range(parts)
        ]
        pieces = total_call(
            functools.partial(total_kernel, row, parts), totals,
            (size, columns), kept["own"][j], got["own"], from_near, from_two,
        )
        row += size
        if parts:
            outs.append(pieces[0])
            outs += [move(pieces[k], "ao", k) for k in range(1, parts)]
        else:
            total = pieces[0].reshape(size, ao_size, own)
            total = jnp.swapaxes(total, 0, 1).reshape(ao_size * size, own)
            value = lax.psum_scatter(total, "ao", scatter_dimension=0, tiled=True)
            outs.append(value.reshape(2, -1, u_own, own))
    if parts:
        result = jax.ShapeDtypeStruct((2, p_own, u_own, own), jnp.float32)
        return small(functools.partial(final_kernel, parts, own), result, *outs)
    return jnp.concatenate(outs, axis=1)


def solution(mesh):
    spec = P(("ao", "gen", "act"), None, None, None)
    count = P(("ao", "gen", "act"))

    def program(integrals, bra_rows, ket_rows, block_count, pair_count):
        mapped = jax.shard_map(
            local,
            mesh=mesh,
            in_specs=(spec, spec, spec, count, count),
            out_specs=P(None, "gen", "act", "ao"),
            check_vma=False,
        )
        return mapped(integrals, bra_rows, ket_rows, block_count, pair_count)

    return program
```

profile of v0, /device:TPU:0, one launch (start us, length us, event | category | flops | bytes accessed | tf_op | source)
XLA Modules:
  0.0 47.4 jit_solution(17531419606394518222)
XLA Ops:
  0.7 0.7 %fusion = bf16[12]{0:T(256)(128)(2,1)S(1)} fusion(s32[12]{0:T(128)} %param.9, s32[]{:T(128)} %bitcast.3), kind=kLoop, calls=%fused_computation.2 | loop fusion | flops 36 | bytes 76 | tf_op jit(solution)/shard_map/convert_element_type | solution.py:395
  1.3 0.1 broadcast_in_dim.11
  1.4 1.0 %pad_maximum_fusion.rows_ref = bf16[12,2,72,128]{3,2,1,0:T(8,128)(2,1)S(1)} fusion(bf16[12,2,8,128]{3,2,1,0:T(8,128)(2,1)S(1)} %broadcast_in_dim.11, bf16[12,2,48,128]{3,2,1,0:T(8,128)(2,1)} %bitcast.4, bf16[12,2,16,128]{3,2,1,0:T(8,128)(2,1)} %bitcast.5), kind=kLoop, calls=%fused_computation | loop fusion | flops 1327104 | bytes 884736 | tf_op jit(solution)/shard_map/concatenate | solution.py:396
  2.4 4.3 %products_0.1 = (bf16[192,1152]{1,0:T(8,128)(2,1)S(1)}, bf16[192,1152]{1,0:T(8,128)(2,1)S(1)}, f32[96,1152]{1,0:T(8,128)S(1)}, f32[96,1152]{1,0:T(8,128)S(1)}, f...) custom-call(bf16[12,2,72,128]{3,2,1,0:T(8,128)(2,1)S(1)} %pad_maximu, ...), custom_call_target="tpu_custom_call" | custom-call | flops 2717908992 | bytes 2654208 | tf_op jit(solution)/shard_map/products_0/pallas_call | solution.py:242
  6.7 1.9 %collective-permute-start.4 = (bf16[192,1152]{1,0:T(8,128)(2,1)S(1)}, bf16[192,1152]{1,0:T(8,128)(2,1)S(1)}, u32[]{:S(2)}, u32[]{:S(2)}) collective-permute-start(bf16[192,1152]{1,0:T(8,128)(2,1)S(1)} %get-tuple-element.39), channel_id=1, source_target_pairs={{0,2},{2,0},{4,6},{6,4},{1,3},{3,1},{5,7},{7,5},{8,10},{10,8},{12,... | collective-permute-start | bytes 1327112 | tf_op jit(solution)/shard_map/ppermute | solution.py:404
  8.6 2.5 %shard_map.55 = (bf16[192,1152]{1,0:T(8,128)(2,1)S(1)}, bf16[192,1152]{1,0:T(8,128)(2,1)S(1)}, f32[96,1152]{1,0:T(8,128)S(1)}, f32[96,1152]{1,0:T(8,128)S(1)}, f...) custom-call(bf16[2,1536,1152]{2,1,0:T(8,128)(2,1)S(1)} %get-tuple-element.28.packed, ...), custom_call_target="tpu_custom_call" | custom-call | flops 452984832 | bytes 2654208 | tf_op jit(solution)/shard_map/pallas_call | solution.py:224
  11.1 1.3 %collective-permute-start.3 = (bf16[192,1152]{1,0:T(8,128)(2,1)S(1)}, bf16[192,1152]{1,0:T(8,128)(2,1)S(1)}, u32[]{:S(2)}, u32[]{:S(2)}) collective-permute-start(bf16[192,1152]{1,0:T(8,128)(2,1)S(1)} %get-tuple-element.36), channel_id=1, source_target_pairs={{0,2},{2,0},{4,6},{6,4},{1,3},{3,1},{5,7},{7,5},{8,10},{10,8},{12,... | collective-permute-start | bytes 1327112 | tf_op jit(solution)/shard_map/ppermute | solution.py:404
  12.4 0.1 collective-permute-start.1
  12.5 0.0 collective-permute-done.4.refs_2_
  12.5 0.1 shard_map.57
  12.6 7.0 %collective-permute-start.5 = (bf16[192,1152]{1,0:T(8,128)(2,1)S(1)}, bf16[192,1152]{1,0:T(8,128)(2,1)S(1)}, u32[]{:S(2)}, u32[]{:S(2)}) collective-permute-start(bf16[192,1152]{1,0:T(8,128)(2,1)S(1)} %shard_map.57), channel_id=1, source_target_pairs={{0,1},{1,0},{2,6},{3,7},{4,5},{5,4},{6,2},{7,3},{8,9},{9,8},{10,14... | collective-permute-start | bytes 1327112 | tf_op jit(solution)/shard_map/ppermute | solution.py:415
  19.6 0.0 collective-permute-start
  19.6 0.0 collective-permute-done.1.got_ref
  19.7 1.8 %collective-permute-start.2 = (bf16[96,1152]{1,0:T(8,128)(2,1)S(1)}, bf16[96,1152]{1,0:T(8,128)(2,1)S(1)}, u32[]{:S(2)}, u32[]{:S(2)}) collective-permute-start(bf16[96,1152]{1,0:T(8,128)(2,1)S(1)} %shard_map.56), channel_id=1, source_target_pairs={{0,1},{1,0},{2,6},{3,7},{4,5},{5,4},{6,2},{7,3},{8,9},{9,8},{10,14... | collective-permute-start | bytes 663560 | tf_op jit(solution)/shard_map/ppermute | solution.py:415
  21.5 4.4 %collective-permute-done.5.from_far = bf16[192,1152]{1,0:T(8,128)(2,1)S(1)} collective-permute-done((bf16[192,1152]{1,0:T(8,128)(2,1)S(1)}, bf16[192,1152]{1,0:T(8,128)(2,1)S(1)}, u32[]{:S(2)}, u32[]{:S(2)}) %collective-permute-start.5) | collective-permute-done | bytes 442400 | tf_op jit(solution)/shard_map/ppermute | solution.py:415
  25.9 0.1 shard_map.58
  26.0 0.1 collective-permute-start.6
  26.1 2.1 %collective-permute-start.10 = (bf16[96,1152]{1,0:T(8,128)(2,1)S(1)}, bf16[96,1152]{1,0:T(8,128)(2,1)S(1)}, u32[]{:S(2)}, u32[]{:S(2)}) collective-permute-start(bf16[96,1152]{1,0:T(8,128)(2,1)S(1)} %shard_map.60), channel_id=1, source_target_pairs={{0,1},{1,0},{2,6},{3,7},{4,5},{5,4},{6,2},{7,3},{8,9},{9,8},{10,14... | collective-permute-start | bytes 663560 | tf_op jit(solution)/shard_map/ppermute | solution.py:415
  28.2 0.1 shard_map.61
  28.3 2.1 %collective-permute-start.11 = (bf16[96,1152]{1,0:T(8,128)(2,1)S(1)}, bf16[96,1152]{1,0:T(8,128)(2,1)S(1)}, u32[]{:S(2)}, u32[]{:S(2)}) collective-permute-start(bf16[96,1152]{1,0:T(8,128)(2,1)S(1)} %shard_map.61), channel_id=1, source_target_pairs={{0,4},{1,5},{2,3},{3,2},{4,0},{5,1},{6,7},{7,6},{8,12},{9,13},{10,... | collective-permute-start | bytes 663560 | tf_op jit(solution)/shard_map/ppermute | solution.py:415
  30.4 3.9 %collective-permute-done.6.from_two = bf16[96,1152]{1,0:T(8,128)(2,1)S(1)} collective-permute-done((bf16[96,1152]{1,0:T(8,128)(2,1)S(1)}, bf16[96,1152]{1,0:T(8,128)(2,1)S(1)}, u32[]{:S(2)}, u32[]{:S(2)}) %collective-permute-start.6) | collective-permute-done | bytes 221216 | tf_op jit(solution)/shard_map/ppermute | solution.py:415
  34.3 0.4 shard_map.59
  34.7 0.0 collective-permute-start.7
  34.7 0.1 collective-permute-start.8
  34.8 4.3 %collective-permute-start.9 = (bf16[216,128]{1,0:T(8,128)(2,1)S(1)}, bf16[216,128]{1,0:T(8,128)(2,1)S(1)}, u32[]{:S(2)}, u32[]{:S(2)}) collective-permute-start(bf16[216,128]{1,0:T(8,128)(2,1)S(1)} %get-tuple-element.43), channel_id=1, source_target_pairs={{0,24},{8,16},{16,8},{24,0},{1,25},{9,17},{17,9},{25,1},{2,26},{10... | collective-permute-start | bytes 165896 | tf_op jit(solution)/shard_map/ppermute | solution.py:404
  39.1 0.4 shard_map.62
  39.5 0.0 collective-permute-start.12
  39.5 0.6 %collective-permute-start.13 = (bf16[216,128]{1,0:T(8,128)(2,1)S(1)}, bf16[216,128]{1,0:T(8,128)(2,1)S(1)}, u32[]{:S(2)}, u32[]{:S(2)}) collective-permute-start(bf16[216,128]{1,0:T(8,128)(2,1)S(1)} %get-tuple-element.49), channel_id=1, source_target_pairs={{0,16},{8,24},{16,0},{24,8},{1,17},{9,25},{17,1},{25,9},{2,18},{10... | collective-permute-start | bytes 165896 | tf_op jit(solution)/shard_map/ppermute | solution.py:404
  40.1 3.8 %collective-permute-start.14 = (bf16[216,128]{1,0:T(8,128)(2,1)S(1)}, bf16[216,128]{1,0:T(8,128)(2,1)S(1)}, u32[]{:S(2)}, u32[]{:S(2)}) collective-permute-start(bf16[216,128]{1,0:T(8,128)(2,1)S(1)} %get-tuple-element.50), channel_id=1, source_target_pairs={{0,24},{8,16},{16,8},{24,0},{1,25},{9,17},{17,9},{25,1},{2,26},{10... | collective-permute-start | bytes 165896 | tf_op jit(solution)/shard_map/ppermute | solution.py:404
  43.9 0.7 %collective-permute-done.13.refs_6_ = bf16[216,128]{1,0:T(8,128)(2,1)S(1)} collective-permute-done((bf16[216,128]{1,0:T(8,128)(2,1)S(1)}, bf16[216,128]{1,0:T(8,128)(2,1)S(1)}, u32[]{:S(2)}, u32[]{:S(2)}) %collective-permute-start.13) | collective-permute-done | bytes 55328 | tf_op jit(solution)/shard_map/ppermute | solution.py:404
  44.6 2.0 %collective-permute-done.14.refs_7_ = bf16[216,128]{1,0:T(8,128)(2,1)S(1)} collective-permute-done((bf16[216,128]{1,0:T(8,128)(2,1)S(1)}, bf16[216,128]{1,0:T(8,128)(2,1)S(1)}, u32[]{:S(2)}, u32[]{:S(2)}) %collective-permute-start.14) | collective-permute-done | bytes 55328 | tf_op jit(solution)/shard_map/ppermute | solution.py:404
  46.6 0.8 %shard_map.63 = f32[2,4,24,288]{3,2,1,0:T(8,128)} custom-call(f32[216,128]{1,0:T(8,128)S(1)} %get-tuple-element.40.refs_0_, bf16[216,128]{1,0:T(8,128)(2,1)S(1)} %collective-permute-done.7.refs_1_, bf16[216,128]{1,0:T(8,128)(2,1)S(1)} %collective-permute-done.8.refs_2_, bf16[216,128]{1,0:T(8,128)(2,1)S(1)} %collective-permute-done.9.refs_3_, ...), custom_call_target="tpu_custom_call" | custom-call | flops 221184 | bytes 884736 | tf_op jit(solution)/shard_map/pallas_call | solution.py:272
  (11 shorter events, 0.1 us)
Async XLA Ops:
  6.7 5.8 %collective-permute-start.4 = (bf16[192,1152]{1,0:T(8,128)(2,1)S(1)}, bf16[192,1152]{1,0:T(8,128)(2,1)S(1)}, u32[]{:S(2)}, u32[]{:S(2)}) collective-permute-start(bf16[192,1152]{1,0:T(8,128)(2,1)S(1)} %get-tuple-element.39), channel_id=1, source_target_pairs={{0,2},{2,0},{4,6},{6,4},{1,3},{3,1},{5,7},{7,5},{8,10},{10,8},{12,... | collective-permute-start | bytes 1327112 | tf_op jit(solution)/shard_map/ppermute | solution.py:404
  11.1 10.4 %collective-permute-start.3 = (bf16[192,1152]{1,0:T(8,128)(2,1)S(1)}, bf16[192,1152]{1,0:T(8,128)(2,1)S(1)}, u32[]{:S(2)}, u32[]{:S(2)}) collective-permute-start(bf16[192,1152]{1,0:T(8,128)(2,1)S(1)} %get-tuple-element.36), channel_id=1, source_target_pairs={{0,2},{2,0},{4,6},{6,4},{1,3},{3,1},{5,7},{7,5},{8,10},{10,8},{12,... | collective-permute-start | bytes 1327112 | tf_op jit(solution)/shard_map/ppermute | solution.py:404
  12.4 7.2 %collective-permute-start.1 = (bf16[192,1152]{1,0:T(8,128)(2,1)S(1)}, bf16[192,1152]{1,0:T(8,128)(2,1)S(1)}, u32[]{:S(2)}, u32[]{:S(2)}) collective-permute-start(bf16[192,1152]{1,0:T(8,128)(2,1)S(1)} %get-tuple-element.34), channel_id=1, source_target_pairs={{0,2},{2,0},{4,6},{6,4},{1,3},{3,1},{5,7},{7,5},{8,10},{10,8},{12,... | collective-permute-start | bytes 1327112 | tf_op jit(solution)/shard_map/ppermute | solution.py:404
  12.6 13.3 %collective-permute-start.5 = (bf16[192,1152]{1,0:T(8,128)(2,1)S(1)}, bf16[192,1152]{1,0:T(8,128)(2,1)S(1)}, u32[]{:S(2)}, u32[]{:S(2)}) collective-permute-start(bf16[192,1152]{1,0:T(8,128)(2,1)S(1)} %shard_map.57), channel_id=1, source_target_pairs={{0,1},{1,0},{2,6},{3,7},{4,5},{5,4},{6,2},{7,3},{8,9},{9,8},{10,14... | collective-permute-start | bytes 1327112 | tf_op jit(solution)/shard_map/ppermute | solution.py:415
  19.6 10.7 %collective-permute-start = (bf16[192,1152]{1,0:T(8,128)(2,1)S(1)}, bf16[192,1152]{1,0:T(8,128)(2,1)S(1)}, u32[]{:S(2)}, u32[]{:S(2)}) collective-permute-start(bf16[192,1152]{1,0:T(8,128)(2,1)S(1)} %get-tuple-element.32), channel_id=1, source_target_pairs={{0,2},{2,0},{4,6},{6,4},{1,3},{3,1},{5,7},{7,5},{8,10},{10,8},{12,... | collective-permute-start | bytes 1327112 | tf_op jit(solution)/shard_map/ppermute | solution.py:404
  19.7 10.7 %collective-permute-start.2 = (bf16[96,1152]{1,0:T(8,128)(2,1)S(1)}, bf16[96,1152]{1,0:T(8,128)(2,1)S(1)}, u32[]{:S(2)}, u32[]{:S(2)}) collective-permute-start(bf16[96,1152]{1,0:T(8,128)(2,1)S(1)} %shard_map.56), channel_id=1, source_target_pairs={{0,1},{1,0},{2,6},{3,7},{4,5},{5,4},{6,2},{7,3},{8,9},{9,8},{10,14... | collective-permute-start | bytes 663560 | tf_op jit(solution)/shard_map/ppermute | solution.py:415
  26.0 8.3 %collective-permute-start.6 = (bf16[96,1152]{1,0:T(8,128)(2,1)S(1)}, bf16[96,1152]{1,0:T(8,128)(2,1)S(1)}, u32[]{:S(2)}, u32[]{:S(2)}) collective-permute-start(bf16[96,1152]{1,0:T(8,128)(2,1)S(1)} %shard_map.58), channel_id=1, source_target_pairs={{0,4},{1,5},{2,3},{3,2},{4,0},{5,1},{6,7},{7,6},{8,12},{9,13},{10,... | collective-permute-start | bytes 663560 | tf_op jit(solution)/shard_map/ppermute | solution.py:415
  26.1 12.9 %collective-permute-start.10 = (bf16[96,1152]{1,0:T(8,128)(2,1)S(1)}, bf16[96,1152]{1,0:T(8,128)(2,1)S(1)}, u32[]{:S(2)}, u32[]{:S(2)}) collective-permute-start(bf16[96,1152]{1,0:T(8,128)(2,1)S(1)} %shard_map.60), channel_id=1, source_target_pairs={{0,1},{1,0},{2,6},{3,7},{4,5},{5,4},{6,2},{7,3},{8,9},{9,8},{10,14... | collective-permute-start | bytes 663560 | tf_op jit(solution)/shard_map/ppermute | solution.py:415
  28.3 10.8 %collective-permute-start.11 = (bf16[96,1152]{1,0:T(8,128)(2,1)S(1)}, bf16[96,1152]{1,0:T(8,128)(2,1)S(1)}, u32[]{:S(2)}, u32[]{:S(2)}) collective-permute-start(bf16[96,1152]{1,0:T(8,128)(2,1)S(1)} %shard_map.61), channel_id=1, source_target_pairs={{0,4},{1,5},{2,3},{3,2},{4,0},{5,1},{6,7},{7,6},{8,12},{9,13},{10,... | collective-permute-start | bytes 663560 | tf_op jit(solution)/shard_map/ppermute | solution.py:415
  34.7 5.4 %collective-permute-start.7 = (bf16[216,128]{1,0:T(8,128)(2,1)S(1)}, bf16[216,128]{1,0:T(8,128)(2,1)S(1)}, u32[]{:S(2)}, u32[]{:S(2)}) collective-permute-start(bf16[216,128]{1,0:T(8,128)(2,1)S(1)} %get-tuple-element.41), channel_id=1, source_target_pairs={{0,8},{8,0},{16,24},{24,16},{1,9},{9,1},{17,25},{25,17},{2,10},{10... | collective-permute-start | bytes 165896 | tf_op jit(solution)/shard_map/ppermute | solution.py:404
  34.7 9.2 %collective-permute-start.8 = (bf16[216,128]{1,0:T(8,128)(2,1)S(1)}, bf16[216,128]{1,0:T(8,128)(2,1)S(1)}, u32[]{:S(2)}, u32[]{:S(2)}) collective-permute-start(bf16[216,128]{1,0:T(8,128)(2,1)S(1)} %get-tuple-element.42), channel_id=1, source_target_pairs={{0,16},{8,24},{16,0},{24,8},{1,17},{9,25},{17,1},{25,9},{2,18},{10... | collective-permute-start | bytes 165896 | tf_op jit(solution)/shard_map/ppermute | solution.py:404
  34.8 9.1 %collective-permute-start.9 = (bf16[216,128]{1,0:T(8,128)(2,1)S(1)}, bf16[216,128]{1,0:T(8,128)(2,1)S(1)}, u32[]{:S(2)}, u32[]{:S(2)}) collective-permute-start(bf16[216,128]{1,0:T(8,128)(2,1)S(1)} %get-tuple-element.43), channel_id=1, source_target_pairs={{0,24},{8,16},{16,8},{24,0},{1,25},{9,17},{17,9},{25,1},{2,26},{10... | collective-permute-start | bytes 165896 | tf_op jit(solution)/shard_map/ppermute | solution.py:404
  39.5 4.4 %collective-permute-start.12 = (bf16[216,128]{1,0:T(8,128)(2,1)S(1)}, bf16[216,128]{1,0:T(8,128)(2,1)S(1)}, u32[]{:S(2)}, u32[]{:S(2)}) collective-permute-start(bf16[216,128]{1,0:T(8,128)(2,1)S(1)} %get-tuple-element.48), channel_id=1, source_target_pairs={{0,8},{8,0},{16,24},{24,16},{1,9},{9,1},{17,25},{25,17},{2,10},{10... | collective-permute-start | bytes 165896 | tf_op jit(solution)/shard_map/ppermute | solution.py:404
  39.5 5.1 %collective-permute-start.13 = (bf16[216,128]{1,0:T(8,128)(2,1)S(1)}, bf16[216,128]{1,0:T(8,128)(2,1)S(1)}, u32[]{:S(2)}, u32[]{:S(2)}) collective-permute-start(bf16[216,128]{1,0:T(8,128)(2,1)S(1)} %get-tuple-element.49), channel_id=1, source_target_pairs={{0,16},{8,24},{16,0},{24,8},{1,17},{9,25},{17,1},{25,9},{2,18},{10... | collective-permute-start | bytes 165896 | tf_op jit(solution)/shard_map/ppermute | solution.py:404
  40.1 6.5 %collective-permute-start.14 = (bf16[216,128]{1,0:T(8,128)(2,1)S(1)}, bf16[216,128]{1,0:T(8,128)(2,1)S(1)}, u32[]{:S(2)}, u32[]{:S(2)}) collective-permute-start(bf16[216,128]{1,0:T(8,128)(2,1)S(1)} %get-tuple-element.50), channel_id=1, source_target_pairs={{0,24},{8,16},{16,8},{24,0},{1,25},{9,17},{17,9},{25,1},{2,26},{10... | collective-permute-start | bytes 165896 | tf_op jit(solution)/shard_map/ppermute | solution.py:404
where the time goes:
time: 47.6 us; the launch traced here: 47.4 us
  starting transfers between devices  25.2 us (53%)
  waiting for transfers between devices  11 us (23%)
  Pallas kernels  8.69 us (18%)
  other arithmetic  1.69 us (4%)
  between operations  0.75 us (2%)
    ppermute x5, starting transfers between devices, cross(): return lax.ppermute(value, ('gen', 'act'), pairs)  13.1 us
    ppermute x10, starting transfers between devices, move(): return lax.ppermute(value, axis, swap(lax.axis_size(axis), bit))  12.1 us
    ppermute x5, waiting for transfers between devices, cross(): return lax.ppermute(value, ('gen', 'act'), pairs)  8.31 us
    pallas_call x1, Pallas kernels, products(): pl.pallas_call(functools.partial(head_kernel, dims, blocks, width), out_s...  4.26 us
    ppermute x10, waiting for transfers between devices, move(): return lax.ppermute(value, axis, swap(lax.axis_size(axis), bit))  2.73 us
    pallas_call x1, Pallas kernels, products(): pl.pallas_call(functools.partial(tail_kernel, dims, chunk), out_shape=out...  2.53 us
    pallas_call x6, Pallas kernels, small(): pl.pallas_call(kernel, out_shape=outs, in_specs=[VMEM] * len(operands), o...  1.1 us
    concatenate x1, other arithmetic, local(): operands = (jnp.concatenate([bra, ket, tail], axis=2), integrals)  1.03 us
  transfers between devices with their start and end apart: 15, of which 4 were waited for; matrix products, arithmetic and copies ran while one was open for 0% of the time, Pallas kernels for 8%

commit v1 on v0

--- a/solution.py
+++ b/solution.py
@@ -284,14 +284,12 @@
 
 
 def total_call(kernel, outs, shape, *operands):
-    scratch = [pltpu.VMEM(shape, jnp.float32)] if outs else []
     outs = outs or [jax.ShapeDtypeStruct(shape, jnp.float32)]
     return pl.pallas_call(
         kernel,
         out_shape=outs,
         in_specs=[VMEM] * len(operands),
         out_specs=[VMEM] * len(outs),
-        scratch_shapes=scratch,
         compiler_params=pltpu.CompilerParams(vmem_limit_bytes=SMALL),
         cost_estimate=pl.CostEstimate(
             flops=sum(x.size for x in operands),
@@ -322,21 +320,26 @@
     out[...] = (value + from_far[row:last].astype(jnp.float32)).astype(out.dtype)
 
 
-def total_kernel(row, parts, own_ref, got_ref, from_near, from_two, *outs):
-    total = outs[-1]
-    last = row + own_ref.shape[0]
-    value = own_ref[...] + got_ref[row:last].astype(jnp.float32)
-    total[...] = value + from_near[...].astype(jnp.float32) + from_two[...].astype(jnp.float32)
+def total_kernel(row, parts, shifts, own_ref, got_ref, from_near, from_two, *outs):
+    rows, columns = own_ref.shape
+    last = row + rows
+
+    def sum_of(lanes):
+        value = own_ref[:, lanes] + got_ref[row:last, lanes].astype(jnp.float32)
+        value = value + from_near[:, lanes].astype(jnp.float32)
+        return value + from_two[:, lanes].astype(jnp.float32)
+
+    if not parts:
+        outs[0][...] = sum_of(slice(None))
     if parts:
-        rows, columns = total.shape
         own, width = window_of(columns, parts)
         full, rest = divmod(own, LANES)
         lane = lax.broadcasted_iota(jnp.int32, (1, LANES), 1)
         me = lax.axis_index("ao")
-        for k, out in enumerate(outs[:-1]):
+        for k, out in zip(shifts, outs):
             first = jnp.minimum((me ^ k) * own // LANES * LANES, columns - width)
             shift = (me ^ k) * own - first
-            cut = total[:, pl.ds(pl.multiple_of(first, LANES), width)]
+            cut = sum_of(pl.ds(pl.multiple_of(first, LANES), width))
             cut = pltpu.roll(cut, jnp.where(shift == 0, 0, width - shift), 1)
             parcels = [cut[:, j * LANES : (j + 1) * LANES] for j in range(full)]
             if rest:
@@ -444,10 +447,17 @@
             jax.ShapeDtypeStruct((dense_rows(own, size), LANES), jnp.bfloat16 if k else jnp.float32)
             for k in range(parts)
         ]
-        pieces = total_call(
-            functools.partial(total_kernel, row, parts), totals,
-            (size, columns), kept["own"][j], got["own"], from_near, from_two,
-        )
+        pieces = [None] * max(parts, 1)
+        for label, shifts in (("lead", [parts - 1]), ("rest", list(range(parts - 1)))):
+            if not parts and label == "rest":
+                continue
+            made = total_call(
+                functools.partial(total_kernel, row, parts, shifts),
+                [totals[k] for k in shifts] if parts else [],
+                (size, columns), kept["own"][j], got["own"], from_near, from_two,
+            )
+            for k, piece in zip(shifts if parts else [0], made):
+                pieces[k] = piece
         row += size
         if parts:
             outs.append(pieces[0])

time: 47.6 us -> 47.6 us (level)
  no operation moved by 1% of the time
where the time goes in v1:
time: 47.6 us; the launch traced here: 47.4 us
  starting transfers between devices  25.3 us (53%)
  waiting for transfers between devices  10.8 us (23%)
  Pallas kernels  8.81 us (19%)
  other arithmetic  1.69 us (4%)
  between operations  0.75 us (2%)
    ppermute x5, starting transfers between devices, cross(): return lax.ppermute(value, ('gen', 'act'), pairs)  13.1 us
    ppermute x10, starting transfers between devices, move(): return lax.ppermute(value, axis, swap(lax.axis_size(axis), bit))  12.3 us
    ppermute x5, waiting for transfers between devices, cross(): return lax.ppermute(value, ('gen', 'act'), pairs)  8.26 us
    pallas_call x1, Pallas kernels, products(): pl.pallas_call(functools.partial(head_kernel, dims, blocks, width), out_s...  4.26 us
    pallas_call x1, Pallas kernels, products(): pl.pallas_call(functools.partial(tail_kernel, dims, chunk), out_shape=out...  2.53 us
    ppermute x10, waiting for transfers between devices, move(): return lax.ppermute(value, axis, swap(lax.axis_size(axis), bit))  2.49 us
    pallas_call x6, Pallas kernels, small(): pl.pallas_call(kernel, out_shape=outs, in_specs=[VMEM] * len(operands), o...  1.16 us
    concatenate x1, other arithmetic, local(): operands = (jnp.concatenate([bra, ket, tail], axis=2), integrals)  1.03 us
  transfers between devices with their start and end apart: 15, of which 4 were waited for; matrix products, arithmetic and copies ran while one was open for 0% of the time, Pallas kernels for 8%

profile of v1, /device:TPU:0, one launch (start us, length us, event | category | flops | bytes accessed | tf_op | source)
XLA Modules:
  0.0 47.4 jit_solution(10995959419400501754)
XLA Ops:
  0.7 0.7 %fusion = bf16[12]{0:T(256)(128)(2,1)S(1)} fusion(s32[12]{0:T(128)} %param.9, s32[]{:T(128)} %bitcast.3), kind=kLoop, calls=%fused_computation.2 | loop fusion | flops 36 | bytes 76 | tf_op jit(solution)/shard_map/convert_element_type | solution.py:398
  1.3 0.1 broadcast_in_dim.11
  1.4 1.0 %pad_maximum_fusion.rows_ref = bf16[12,2,72,128]{3,2,1,0:T(8,128)(2,1)S(1)} fusion(bf16[12,2,8,128]{3,2,1,0:T(8,128)(2,1)S(1)} %broadcast_in_dim.11, bf16[12,2,48,128]{3,2,1,0:T(8,128)(2,1)} %bitcast.4, bf16[12,2,16,128]{3,2,1,0:T(8,128)(2,1)} %bitcast.5), kind=kLoop, calls=%fused_computation | loop fusion | flops 1327104 | bytes 884736 | tf_op jit(solution)/shard_map/concatenate | solution.py:399
  2.4 4.3 %products_0.1 = (bf16[192,1152]{1,0:T(8,128)(2,1)S(1)}, bf16[192,1152]{1,0:T(8,128)(2,1)S(1)}, f32[96,1152]{1,0:T(8,128)S(1)}, f32[96,1152]{1,0:T(8,128)S(1)}, f...) custom-call(bf16[12,2,72,128]{3,2,1,0:T(8,128)(2,1)S(1)} %pad_maximu, ...), custom_call_target="tpu_custom_call" | custom-call | flops 2717908992 | bytes 2654208 | tf_op jit(solution)/shard_map/products_0/pallas_call | solution.py:242
  6.7 1.9 %collective-permute-start.4 = (bf16[192,1152]{1,0:T(8,128)(2,1)S(1)}, bf16[192,1152]{1,0:T(8,128)(2,1)S(1)}, u32[]{:S(2)}, u32[]{:S(2)}) collective-permute-start(bf16[192,1152]{1,0:T(8,128)(2,1)S(1)} %get-tuple-element.37), channel_id=1, source_target_pairs={{0,2},{2,0},{4,6},{6,4},{1,3},{3,1},{5,7},{7,5},{8,10},{10,8},{12,... | collective-permute-start | bytes 1327112 | tf_op jit(solution)/shard_map/ppermute | solution.py:407
  8.6 2.5 %shard_map.55 = (bf16[192,1152]{1,0:T(8,128)(2,1)S(1)}, bf16[192,1152]{1,0:T(8,128)(2,1)S(1)}, f32[96,1152]{1,0:T(8,128)S(1)}, f32[96,1152]{1,0:T(8,128)S(1)}, f...) custom-call(bf16[2,1536,1152]{2,1,0:T(8,128)(2,1)S(1)} %get-tuple-element.26.packed, ...), custom_call_target="tpu_custom_call" | custom-call | flops 452984832 | bytes 2654208 | tf_op jit(solution)/shard_map/pallas_call | solution.py:224
  11.1 1.3 %collective-permute-start.3 = (bf16[192,1152]{1,0:T(8,128)(2,1)S(1)}, bf16[192,1152]{1,0:T(8,128)(2,1)S(1)}, u32[]{:S(2)}, u32[]{:S(2)}) collective-permute-start(bf16[192,1152]{1,0:T(8,128)(2,1)S(1)} %get-tuple-element.34), channel_id=1, source_target_pairs={{0,2},{2,0},{4,6},{6,4},{1,3},{3,1},{5,7},{7,5},{8,10},{10,8},{12,... | collective-permute-start | bytes 1327112 | tf_op jit(solution)/shard_map/ppermute | solution.py:407
  12.4 0.1 collective-permute-start.1
  12.5 0.1 shard_map.57
  12.6 7.0 %collective-permute-start.5 = (bf16[192,1152]{1,0:T(8,128)(2,1)S(1)}, bf16[192,1152]{1,0:T(8,128)(2,1)S(1)}, u32[]{:S(2)}, u32[]{:S(2)}) collective-permute-start(bf16[192,1152]{1,0:T(8,128)(2,1)S(1)} %shard_map.57), channel_id=1, source_target_pairs={{0,1},{1,0},{2,6},{3,7},{4,5},{5,4},{6,2},{7,3},{8,9},{9,8},{10,14... | collective-permute-start | bytes 1327112 | tf_op jit(solution)/shard_map/ppermute | solution.py:418
  19.7 1.8 %collective-permute-start.2 = (bf16[96,1152]{1,0:T(8,128)(2,1)S(1)}, bf16[96,1152]{1,0:T(8,128)(2,1)S(1)}, u32[]{:S(2)}, u32[]{:S(2)}) collective-permute-start(bf16[96,1152]{1,0:T(8,128)(2,1)S(1)} %shard_map.56), channel_id=1, source_target_pairs={{0,1},{1,0},{2,6},{3,7},{4,5},{5,4},{6,2},{7,3},{8,9},{9,8},{10,14... | collective-permute-start | bytes 663560 | tf_op jit(solution)/shard_map/ppermute | solution.py:418
  21.5 4.4 %collective-permute-done.5.from_far = bf16[192,1152]{1,0:T(8,128)(2,1)S(1)} collective-permute-done((bf16[192,1152]{1,0:T(8,128)(2,1)S(1)}, bf16[192,1152]{1,0:T(8,128)(2,1)S(1)}, u32[]{:S(2)}, u32[]{:S(2)}) %collective-permute-start.5) | collective-permute-done | bytes 442400 | tf_op jit(solution)/shard_map/ppermute | solution.py:418
  25.9 0.1 shard_map.58
  26.0 0.1 collective-permute-start.6
  26.1 0.1 shard_map.61
  26.1 2.1 %collective-permute-start.10 = (bf16[96,1152]{1,0:T(8,128)(2,1)S(1)}, bf16[96,1152]{1,0:T(8,128)(2,1)S(1)}, u32[]{:S(2)}, u32[]{:S(2)}) collective-permute-start(bf16[96,1152]{1,0:T(8,128)(2,1)S(1)} %shard_map.61), channel_id=1, source_target_pairs={{0,1},{1,0},{2,6},{3,7},{4,5},{5,4},{6,2},{7,3},{8,9},{9,8},{10,14... | collective-permute-start | bytes 663560 | tf_op jit(solution)/shard_map/ppermute | solution.py:418
  28.2 0.1 shard_map.62
  28.3 2.1 %collective-permute-start.11 = (bf16[96,1152]{1,0:T(8,128)(2,1)S(1)}, bf16[96,1152]{1,0:T(8,128)(2,1)S(1)}, u32[]{:S(2)}, u32[]{:S(2)}) collective-permute-start(bf16[96,1152]{1,0:T(8,128)(2,1)S(1)} %shard_map.62), channel_id=1, source_target_pairs={{0,4},{1,5},{2,3},{3,2},{4,0},{5,1},{6,7},{7,6},{8,12},{9,13},{10,... | collective-permute-start | bytes 663560 | tf_op jit(solution)/shard_map/ppermute | solution.py:418
  30.4 3.9 %collective-permute-done.6.from_two = bf16[96,1152]{1,0:T(8,128)(2,1)S(1)} collective-permute-done((bf16[96,1152]{1,0:T(8,128)(2,1)S(1)}, bf16[96,1152]{1,0:T(8,128)(2,1)S(1)}, u32[]{:S(2)}, u32[]{:S(2)}) %collective-permute-start.6) | collective-permute-done | bytes 221216 | tf_op jit(solution)/shard_map/ppermute | solution.py:418
  34.3 0.2 shard_map.59
  34.5 0.1 collective-permute-start.7
  34.6 0.1 collective-permute-start.8
  34.7 0.2 shard_map.60
  34.9 4.3 %collective-permute-start.9 = (bf16[216,128]{1,0:T(8,128)(2,1)S(1)}, bf16[216,128]{1,0:T(8,128)(2,1)S(1)}, u32[]{:S(2)}, u32[]{:S(2)}) collective-permute-start(bf16[216,128]{1,0:T(8,128)(2,1)S(1)} %shard_map.60), channel_id=1, source_target_pairs={{0,24},{8,16},{16,8},{24,0},{1,25},{9,17},{17,9},{25,1},{2,26},{10... | collective-permute-start | bytes 165896 | tf_op jit(solution)/shard_map/ppermute | solution.py:407
  39.2 0.2 shard_map.63
  39.4 0.1 collective-permute-start.12
  39.5 0.6 %collective-permute-start.13 = (bf16[216,128]{1,0:T(8,128)(2,1)S(1)}, bf16[216,128]{1,0:T(8,128)(2,1)S(1)}, u32[]{:S(2)}, u32[]{:S(2)}) collective-permute-start(bf16[216,128]{1,0:T(8,128)(2,1)S(1)} %get-tuple-element.46), channel_id=1, source_target_pairs={{0,16},{8,24},{16,0},{24,8},{1,17},{9,25},{17,1},{25,9},{2,18},{10... | collective-permute-start | bytes 165896 | tf_op jit(solution)/shard_map/ppermute | solution.py:407
  40.1 0.2 shard_map.64
  40.3 3.9 %collective-permute-start.14 = (bf16[216,128]{1,0:T(8,128)(2,1)S(1)}, bf16[216,128]{1,0:T(8,128)(2,1)S(1)}, u32[]{:S(2)}, u32[]{:S(2)}) collective-permute-start(bf16[216,128]{1,0:T(8,128)(2,1)S(1)} %shard_map.64), channel_id=1, source_target_pairs={{0,24},{8,16},{16,8},{24,0},{1,25},{9,17},{17,9},{25,1},{2,26},{10... | collective-permute-start | bytes 165896 | tf_op jit(solution)/shard_map/ppermute | solution.py:407
  44.1 0.5 %collective-permute-done.13.refs_6_ = bf16[216,128]{1,0:T(8,128)(2,1)S(1)} collective-permute-done((bf16[216,128]{1,0:T(8,128)(2,1)S(1)}, bf16[216,128]{1,0:T(8,128)(2,1)S(1)}, u32[]{:S(2)}, u32[]{:S(2)}) %collective-permute-start.13) | collective-permute-done | bytes 55328 | tf_op jit(solution)/shard_map/ppermute | solution.py:407
  44.6 2.0 %collective-permute-done.14.refs_7_ = bf16[216,128]{1,0:T(8,128)(2,1)S(1)} collective-permute-done((bf16[216,128]{1,0:T(8,128)(2,1)S(1)}, bf16[216,128]{1,0:T(8,128)(2,1)S(1)}, u32[]{:S(2)}, u32[]{:S(2)}) %collective-permute-start.14) | collective-permute-done | bytes 55328 | tf_op jit(solution)/shard_map/ppermute | solution.py:407
  46.6 0.8 %shard_map.65 = f32[2,4,24,288]{3,2,1,0:T(8,128)} custom-call(f32[216,128]{1,0:T(8,128)S(1)} %get-tuple-element.38.refs_0_, bf16[216,128]{1,0:T(8,128)(2,1)S(1)} %collective-permute-done.7.refs_1_, bf16[216,128]{1,0:T(8,128)(2,1)S(1)} %collective-permute-done.8.refs_2_, bf16[216,128]{1,0:T(8,128)(2,1)S(1)} %collective-permute-done.9.refs_3_, ...), custom_call_target="tpu_custom_call" | custom-call | flops 221184 | bytes 884736 | tf_op jit(solution)/shard_map/pallas_call | solution.py:272
  (13 shorter events, 0.1 us)
Async XLA Ops:
  6.7 5.8 %collective-permute-start.4 = (bf16[192,1152]{1,0:T(8,128)(2,1)S(1)}, bf16[192,1152]{1,0:T(8,128)(2,1)S(1)}, u32[]{:S(2)}, u32[]{:S(2)}) collective-permute-start(bf16[192,1152]{1,0:T(8,128)(2,1)S(1)} %get-tuple-element.37), channel_id=1, source_target_pairs={{0,2},{2,0},{4,6},{6,4},{1,3},{3,1},{5,7},{7,5},{8,10},{10,8},{12,... | collective-permute-start | bytes 1327112 | tf_op jit(solution)/shard_map/ppermute | solution.py:407
  11.1 10.4 %collective-permute-start.3 = (bf16[192,1152]{1,0:T(8,128)(2,1)S(1)}, bf16[192,1152]{1,0:T(8,128)(2,1)S(1)}, u32[]{:S(2)}, u32[]{:S(2)}) collective-permute-start(bf16[192,1152]{1,0:T(8,128)(2,1)S(1)} %get-tuple-element.34), channel_id=1, source_target_pairs={{0,2},{2,0},{4,6},{6,4},{1,3},{3,1},{5,7},{7,5},{8,10},{10,8},{12,... | collective-permute-start | bytes 1327112 | tf_op jit(solution)/shard_map/ppermute | solution.py:407
  12.4 7.2 %collective-permute-start.1 = (bf16[192,1152]{1,0:T(8,128)(2,1)S(1)}, bf16[192,1152]{1,0:T(8,128)(2,1)S(1)}, u32[]{:S(2)}, u32[]{:S(2)}) collective-permute-start(bf16[192,1152]{1,0:T(8,128)(2,1)S(1)} %get-tuple-element.32), channel_id=1, source_target_pairs={{0,2},{2,0},{4,6},{6,4},{1,3},{3,1},{5,7},{7,5},{8,10},{10,8},{12,... | collective-permute-start | bytes 1327112 | tf_op jit(solution)/shard_map/ppermute | solution.py:407
  12.6 13.3 %collective-permute-start.5 = (bf16[192,1152]{1,0:T(8,128)(2,1)S(1)}, bf16[192,1152]{1,0:T(8,128)(2,1)S(1)}, u32[]{:S(2)}, u32[]{:S(2)}) collective-permute-start(bf16[192,1152]{1,0:T(8,128)(2,1)S(1)} %shard_map.57), channel_id=1, source_target_pairs={{0,1},{1,0},{2,6},{3,7},{4,5},{5,4},{6,2},{7,3},{8,9},{9,8},{10,14... | collective-permute-start | bytes 1327112 | tf_op jit(solution)/shard_map/ppermute | solution.py:418
  19.6 10.8 %collective-permute-start = (bf16[192,1152]{1,0:T(8,128)(2,1)S(1)}, bf16[192,1152]{1,0:T(8,128)(2,1)S(1)}, u32[]{:S(2)}, u32[]{:S(2)}) collective-permute-start(bf16[192,1152]{1,0:T(8,128)(2,1)S(1)} %get-tuple-element.30), channel_id=1, source_target_pairs={{0,2},{2,0},{4,6},{6,4},{1,3},{3,1},{5,7},{7,5},{8,10},{10,8},{12,... | collective-permute-start | bytes 1327112 | tf_op jit(solution)/shard_map/ppermute | solution.py:407
  19.7 10.7 %collective-permute-start.2 = (bf16[96,1152]{1,0:T(8,128)(2,1)S(1)}, bf16[96,1152]{1,0:T(8,128)(2,1)S(1)}, u32[]{:S(2)}, u32[]{:S(2)}) collective-permute-start(bf16[96,1152]{1,0:T(8,128)(2,1)S(1)} %shard_map.56), channel_id=1, source_target_pairs={{0,1},{1,0},{2,6},{3,7},{4,5},{5,4},{6,2},{7,3},{8,9},{9,8},{10,14... | collective-permute-start | bytes 663560 | tf_op jit(solution)/shard_map/ppermute | solution.py:418
  26.0 8.3 %collective-permute-start.6 = (bf16[96,1152]{1,0:T(8,128)(2,1)S(1)}, bf16[96,1152]{1,0:T(8,128)(2,1)S(1)}, u32[]{:S(2)}, u32[]{:S(2)}) collective-permute-start(bf16[96,1152]{1,0:T(8,128)(2,1)S(1)} %shard_map.58), channel_id=1, source_target_pairs={{0,4},{1,5},{2,3},{3,2},{4,0},{5,1},{6,7},{7,6},{8,12},{9,13},{10,... | collective-permute-start | bytes 663560 | tf_op jit(solution)/shard_map/ppermute | solution.py:418
  26.1 13.0 %collective-permute-start.10 = (bf16[96,1152]{1,0:T(8,128)(2,1)S(1)}, bf16[96,1152]{1,0:T(8,128)(2,1)S(1)}, u32[]{:S(2)}, u32[]{:S(2)}) collective-permute-start(bf16[96,1152]{1,0:T(8,128)(2,1)S(1)} %shard_map.61), channel_id=1, source_target_pairs={{0,1},{1,0},{2,6},{3,7},{4,5},{5,4},{6,2},{7,3},{8,9},{9,8},{10,14... | collective-permute-start | bytes 663560 | tf_op jit(solution)/shard_map/ppermute | solution.py:418
  28.3 10.9 %collective-permute-start.11 = (bf16[96,1152]{1,0:T(8,128)(2,1)S(1)}, bf16[96,1152]{1,0:T(8,128)(2,1)S(1)}, u32[]{:S(2)}, u32[]{:S(2)}) collective-permute-start(bf16[96,1152]{1,0:T(8,128)(2,1)S(1)} %shard_map.62), channel_id=1, source_target_pairs={{0,4},{1,5},{2,3},{3,2},{4,0},{5,1},{6,7},{7,6},{8,12},{9,13},{10,... | collective-permute-start | bytes 663560 | tf_op jit(solution)/shard_map/ppermute | solution.py:418
  34.5 5.8 %collective-permute-start.7 = (bf16[216,128]{1,0:T(8,128)(2,1)S(1)}, bf16[216,128]{1,0:T(8,128)(2,1)S(1)}, u32[]{:S(2)}, u32[]{:S(2)}) collective-permute-start(bf16[216,128]{1,0:T(8,128)(2,1)S(1)} %get-tuple-element.39), channel_id=1, source_target_pairs={{0,8},{8,0},{16,24},{24,16},{1,9},{9,1},{17,25},{25,17},{2,10},{10... | collective-permute-start | bytes 165896 | tf_op jit(solution)/shard_map/ppermute | solution.py:407
  34.6 9.6 %collective-permute-start.8 = (bf16[216,128]{1,0:T(8,128)(2,1)S(1)}, bf16[216,128]{1,0:T(8,128)(2,1)S(1)}, u32[]{:S(2)}, u32[]{:S(2)}) collective-permute-start(bf16[216,128]{1,0:T(8,128)(2,1)S(1)} %get-tuple-element.40), channel_id=1, source_target_pairs={{0,16},{8,24},{16,0},{24,8},{1,17},{9,25},{17,1},{25,9},{2,18},{10... | collective-permute-start | bytes 165896 | tf_op jit(solution)/shard_map/ppermute | solution.py:407
  34.9 9.3 %collective-permute-start.9 = (bf16[216,128]{1,0:T(8,128)(2,1)S(1)}, bf16[216,128]{1,0:T(8,128)(2,1)S(1)}, u32[]{:S(2)}, u32[]{:S(2)}) collective-permute-start(bf16[216,128]{1,0:T(8,128)(2,1)S(1)} %shard_map.60), channel_id=1, source_target_pairs={{0,24},{8,16},{16,8},{24,0},{1,25},{9,17},{17,9},{25,1},{2,26},{10... | collective-permute-start | bytes 165896 | tf_op jit(solution)/shard_map/ppermute | solution.py:407
  39.4 4.7 %collective-permute-start.12 = (bf16[216,128]{1,0:T(8,128)(2,1)S(1)}, bf16[216,128]{1,0:T(8,128)(2,1)S(1)}, u32[]{:S(2)}, u32[]{:S(2)}) collective-permute-start(bf16[216,128]{1,0:T(8,128)(2,1)S(1)} %get-tuple-element.45), channel_id=1, source_target_pairs={{0,8},{8,0},{16,24},{24,16},{1,9},{9,1},{17,25},{25,17},{2,10},{10... | collective-permute-start | bytes 165896 | tf_op jit(solution)/shard_map/ppermute | solution.py:407
  39.5 5.1 %collective-permute-start.13 = (bf16[216,128]{1,0:T(8,128)(2,1)S(1)}, bf16[216,128]{1,0:T(8,128)(2,1)S(1)}, u32[]{:S(2)}, u32[]{:S(2)}) collective-permute-start(bf16[216,128]{1,0:T(8,128)(2,1)S(1)} %get-tuple-element.46), channel_id=1, source_target_pairs={{0,16},{8,24},{16,0},{24,8},{1,17},{9,25},{17,1},{25,9},{2,18},{10... | collective-permute-start | bytes 165896 | tf_op jit(solution)/shard_map/ppermute | solution.py:407
  40.3 6.3 %collective-permute-start.14 = (bf16[216,128]{1,0:T(8,128)(2,1)S(1)}, bf16[216,128]{1,0:T(8,128)(2,1)S(1)}, u32[]{:S(2)}, u32[]{:S(2)}) collective-permute-start(bf16[216,128]{1,0:T(8,128)(2,1)S(1)} %shard_map.64), channel_id=1, source_target_pairs={{0,24},{8,16},{16,8},{24,0},{1,25},{9,17},{17,9},{25,1},{2,26},{10... | collective-permute-start | bytes 165896 | tf_op jit(solution)/shard_map/ppermute | solution.py:407
